TPU v7x, 256 devices: a whole 4x4x8 slice. The times are simulated.
256 devices in a mesh: dp: 16 (over z_hi, x, core), space: 16 (over z_lo, y).
Axes of the slice: x: 4, y: 4, z: 8 (z_hi: 2, z_lo: 4; z = z_hi * 4 + z_lo), core: 2. Of those that a mesh axis runs over, the one named last changes fastest.
Arguments:
- volume: bfloat16 [16, 4, 128, 8, 256], P('dp', None, 'space'), may hold values from -6 to 6
- first_filters: bfloat16 [16, 4, 3, 3, 3], replicated, may hold values from -0.625 to 0.625
- first_biases: float32 [16], replicated, may hold values from -0.5 to 0.5
- second_filters: bfloat16 [32, 16, 3, 3, 3], replicated, may hold values from -0.3125 to 0.3125
- second_biases: float32 [32], replicated, may hold values from -0.5 to 0.5
- cotangent: bfloat16 [16, 32, 64, 4, 128], P('dp', None, 'space'), may hold values from -12 to 12
Outputs:
- activations: bfloat16 [16, 32, 64, 4, 128], P('dp', None, 'space')
- pooled_grad: bfloat16 [16, 16, 64, 4, 128], P('dp', None, 'space')
- gradient_one: float32 [16, 4, 3, 3, 3], replicated
- shift_one: float32 [16], replicated
- gradient_two: float32 [32, 16, 3, 3, 3], replicated
- shift_two: float32 [32], replicated
All inputs are finite; a program needn't handle non-finite values.
Results may differ from a plain program's by a relative error of at most 0.015.
The roundings to bfloat16 on the way count: a program that leaves them out, or rounds other values in their place, can miss the bound.
Values may be sent and summed in bfloat16 or wider, within the bound.
No kernel may reach another device: no remote copies, remote signals or barrier semaphores. Data moves between devices by JAX's collectives and lax.ppermute only.
A program may use at most 128 MiB of HBM per device.

v0:
```python
import math
import jax
import jax.numpy as jnp
from jax import lax
from jax.sharding import PartitionSpec as P


def with_halo(block, sides, width):
    for axis, dim in sides:
        count = lax.axis_size(axis)
        forward = [(i, i + 1) for i in range(count - 1)]
        backward = [(target, source) for source, target in forward]
        low = lax.ppermute(
            lax.slice_in_dim(block, block.shape[dim] - width, None, axis=dim), axis, forward
        )
        high = lax.ppermute(lax.slice_in_dim(block, 0, width, axis=dim), axis, backward)
        block = jnp.concatenate([low, block, high], axis=dim)
    return block


def convolve(padded, kernel):
    return lax.conv_general_dilated(
        padded[None],
        kernel,
        (1, 1, 1),
        "VALID",
        dimension_numbers=("NCDHW", "OIDHW", "NCDHW"),
        preferred_element_type=jnp.float32,
    )[0]


def kernel_grad(padded, errors):
    result = lax.conv_general_dilated(
        padded[:, None],
        errors[:, None],
        (1, 1, 1),
        "VALID",
        dimension_numbers=("NCDHW", "OIDHW", "NCDHW"),
        preferred_element_type=jnp.float32,
    )
    return result.transpose(1, 0, 2, 3, 4)


def pad_plane(values):
    return jnp.pad(values, ((0, 0), (0, 0), (1, 1), (1, 1)))


def leaky_rectify(values):
    return jnp.where(values > 0, values, 0.3 * values)


def rectify_slope(values):
    return jnp.where(values > 0, 1.0, 0.3)


def mean_pool(values):
    extent = values.shape
    blocks = values.reshape(extent[0], extent[1] // 2, 2, extent[2] // 2, 2, extent[3] // 2, 2)
    return jnp.sum(blocks, axis=(2, 4, 6)) * 0.125


def spread_up(values):
    extent = values.shape
    grown = jnp.broadcast_to(
        values[:, :, None, :, None, :, None], (extent[0], extent[1], 2, extent[2], 2, extent[3], 2)
    )
    return grown.reshape(extent[0], 2 * extent[1], 2 * extent[2], 2 * extent[3])


def shards(volume, first_filters, first_biases, second_filters, second_biases, cotangent):
    sample = volume[0]
    target = cotangent[0]
    planes = sample.shape[1]
    rim_depth = 1
    haloed = with_halo(sample, (("space", 1),), 1)
    first_in = pad_plane(haloed)
    linear_one = convolve(first_in, first_filters) + first_biases[:, None, None, None]
    pooled = mean_pool(leaky_rectify(linear_one)).astype(jnp.bfloat16)
    pooled_ext = with_halo(pooled, (("space", 1),), rim_depth)
    second_in = pad_plane(pooled_ext)
    linear_wide = convolve(second_in, second_filters) + second_biases[:, None, None, None]
    delta_two = (target.astype(jnp.float32) * rectify_slope(linear_wide)).astype(jnp.bfloat16)
    delta_ext = with_halo(delta_two, (("space", 1),), 1)
    activations = leaky_rectify(linear_wide).astype(jnp.bfloat16)
    second_terms = (
        kernel_grad(second_in, delta_two),
        jnp.sum(delta_two.astype(jnp.float32), axis=(1, 2, 3)),
    )
    second_terms = lax.psum((second_terms[0], second_terms[1]), ("dp", "space"))
    flipped = jnp.flip(second_filters, (2, 3, 4)).transpose(1, 0, 2, 3, 4)
    pooled_grad = convolve(pad_plane(delta_ext), flipped).astype(jnp.bfloat16)
    stored_grad = lax.optimization_barrier(pooled_grad)
    delta_one = (
        spread_up(stored_grad.astype(jnp.float32)) * 0.125 * rectify_slope(linear_one)
    ).astype(jnp.bfloat16)
    first_terms = (
        kernel_grad(first_in, delta_one),
        jnp.sum(delta_one.astype(jnp.float32), axis=(1, 2, 3)),
    )
    first_terms = lax.psum((first_terms[0], first_terms[1]), ("dp", "space"))
    totals = (first_terms[0], first_terms[1], second_terms[0], second_terms[1])
    count_one = (
        lax.axis_size("dp") * lax.axis_size("space") * planes * sample.shape[2] * sample.shape[3]
    )
    scale_one = 1.0 / math.sqrt(count_one)
    scale_two = 1.0 / math.sqrt(count_one / 8)
    return (
        activations[None],
        pooled_grad[None],
        totals[0] * scale_one,
        totals[1] * scale_one,
        totals[2] * scale_two,
        totals[3] * scale_two,
    )


def solution(mesh):
    placed = (
        P("dp", None, "space", None, None),
        P(),
        P(),
        P(),
        P(),
        P("dp", None, "space", None, None),
    )
    return jax.shard_map(
        shards,
        mesh=mesh,
        in_specs=placed,
        out_specs=(
            P("dp", None, "space", None, None),
            P("dp", None, "space", None, None),
            P(),
            P(),
            P(),
            P(),
        ),
        check_vma=False,
    )
```

profile of v0, /device:TPU:1, one launch (start us, length us, event | category | flops | bytes accessed | tf_op | source)
XLA Modules:
  0.0 488.8 jit_solution(2869849680273263854)
XLA Ops:
  1.4 4.0 collective-permute-start
  5.4 1.3 collective-permute-start.1
  6.7 1.3 copy.164
  8.1 1.8 collective-permute-done.1
  9.9 1.3 fusion.79
  12.1 4.3 copy.155
  17.6 25.4 %fusion = (f32[8,8,8,33,16]{4,2,3,1,0:T(8,128)}, f32[8,8,8,33,16]{4,2,3,1,0:T(8,128)}) fusion(f32[16]{0:T(128)S(1)} %copy-done.12, bf16[16,4,3,3,3]{0,1,4,3,2:T(4,128)(2,1)S(1)} %copy-done.16, bf16[4,10,10,1,7,2]{4,0,5,2,1,3:T(4,128)(2,1)S(1)} %slice.34, bf16[4,10,10,1,8,33]{4,0,5,2,1,3:T(4,128)(2,1)} %copy.155, pred[8,33]{0,1:T(8,128)(4,1)S(1)} %copy-done.17), kind=kOutput, calls=%fused_computation.2 | convolution fusion | flops 60145920 | bytes 2388872 | tf_op jit(solution)/shard_map/conv_general_dilated | solution.py:22
  43.0 8.5 %copy.156 = f32[8,8,8,33,16]{3,2,4,1,0:T(8,128)} copy(f32[8,8,8,33,16]{4,2,3,1,0:T(8,128)} %get-tuple-element.65) | data formatting | bytes 2162688 | tf_op jit(solution)/shard_map/conv_general_dilated | solution.py:22
  51.5 3.5 reshape.99
  55.1 4.8 copy.157
  60.0 12.8 %fusion.2 = f32[16,4,4,128]{0,3,2,1:T(8,128)S(1)} fusion(f32[16,4,2,4,2,128,2]{0,6,5,4,3,2,1:T(2,128)} %bitcast.110, f32[16]{0:T(128)S(1)} %copy-done.12), kind=kLoop, calls=%fused_computation.6 | loop fusion | flops 1277952 | bytes 1179712 | tf_op jit(solution)/shard_map/reduce_sum | solution.py:59
  73.6 3.9 collective-permute-start.2
  77.5 1.3 collective-permute-start.3
  80.1 9.0 %copy.178 = f32[8,8,8,33,16]{3,2,4,1,0:T(8,128)} copy(f32[8,8,8,33,16]{4,2,3,1,0:T(8,128)} %get-tuple-element.64) | data formatting | bytes 2162688 | tf_op jit(solution)/shard_map/jit(_where)/select_n | solution.py:53
  89.2 3.5 reshape.117
  92.8 4.6 copy.190
  97.3 29.6 %copy.176 = bf16[4,1,10,10,258]{0,1,4,3,2:T(2,128)(2,1)} copy(bf16[4,1,10,10,258]{4,3,2,0,1:T(8,128)(2,1)S(1)} %copy-done.6) | data formatting | bytes 412800 | tf_op jit(solution)/shard_map/broadcast_in_dim | solution.py:34
  129.9 2.0 copy.162
  132.1 2.8 fusion.36
  137.5 2.5 copy.180
  140.2 4.0 collective-permute-start.4
  144.2 1.5 collective-permute-start.5
  146.9 16.5 %fusion.44 = f32[32,16,3,3,3]{0,1,4,3,2:T(8,128)} fusion(bf16[16,1,6,6,130]{0,1,4,3,2:T(2,128)(2,1)S(1)} %copy.180, bf16[32,1,4,4,128]{0,3,4,2,1:T(4,128)(2,1)} %fusion.40), kind=kOutput, calls=%fused_computation.64 | convolution fusion | flops 56623104 | bytes 336128 | tf_op jit(solution)/shard_map/transpose | solution.py:41
  165.4 1.7 reshape.111
  167.2 3.0 copy.170
  171.1 3.2 fusion.18
  177.7 7.4 %broadcast_in_dim.50 = f32[16,4,2,4,2,128,2]{0,6,5,4,3,2,1:T(2,128)} broadcast(f32[16,4,4,128]{0,3,2,1:T(8,128)S(1)} %convert_multiply_fusion), dimensions={0,1,3,5} | broadcast | bytes 1179648 | tf_op jit(solution)/shard_map/broadcast_in_dim | solution.py:64
  185.1 5.2 %copy.175 = f32[16,1,8,8,256]{4,0,3,2,1:T(8,128)S(1)} copy(f32[16,1,8,8,256]{0,4,3,2,1:T(8,128)} %bitcast.108) | data formatting | bytes 2097152 | tf_op jit(solution)/shard_map/mul | solution.py:94
  190.6 14.3 %copy.177 = bf16[16,1,8,8,256]{0,1,4,3,2:T(2,128)(2,1)} copy(bf16[16,1,8,8,256]{4,0,3,2,1:T(8,128)(2,1)S(1)} %multiply_convert_fusion) | data formatting | bytes 1048576 | tf_op jit(solution)/shard_map/convert_element_type | solution.py:95
  204.9 8.6 %convert_reduce_fusion = f32[16]{0:T(128)} fusion(f32[1,16,8,8,256]{1,4,3,2,0:T(8,128)} %bitcast.109, f32[8,8,1,256,16]{4,3,1,0,2:T(8,128)} %copy.190), kind=kLoop, calls=%fused_computation.5 | loop fusion | flops 1048560 | bytes 2097216 | tf_op jit(solution)/shard_map/reduce_sum | solution.py:98
  213.6 183.3 %fusion.81 = f32[16,4,3,3,3]{0,1,4,3,2:T(4,128)S(1)} fusion(bf16[4,1,10,10,258]{0,1,4,3,2:T(2,128)(2,1)} %copy.176, bf16[16,1,8,8,256]{0,1,4,3,2:T(2,128)(2,1)S(1)} %copy-done.4), kind=kOutput, calls=%fused_computation.118 | convolution fusion | flops 56623104 | bytes 737600 | tf_op jit(solution)/shard_map/transpose | solution.py:41
  396.9 88.3 %all-reduce.3 = (f32[16,4,3,3,3]{0,1,4,3,2:T(4,128)S(1)}, f32[16]{0:T(128)S(1)}, f32[32,16,3,3,3]{0,1,4,3,2:T(8,128)S(1)}, f32[32]{0:T(128)S(1)}) all-reduce(f32[16,4,3,3,3]{0,1,4,3,2:T(4,128)S(1)} %fusion.81, f32[16]{0:T(128)S(1)} %copy-done.10, ...), channel_id=1, replica_groups=mesh['dp'=16,'space'=16] {'dp','space'}, use_global_device_ids=true, to_apply=%region_1.2 | all-reduce | flops 15600 | bytes 124800 | tf_op jit(solution)/shard_map/psum | solution.py:100
  (85 shorter events, 21.9 us)
Async XLA Ops:
  0.6 131.4 %copy-start = (bf16[32,16,3,3,3]{0,1,4,3,2:T(8,128)(2,1)S(1)}, bf16[32,16,3,3,3]{0,1,4,3,2:T(8,128)(2,1)}, u32[]{:S(2)}) copy-start(bf16[32,16,3,3,3]{0,1,4,3,2:T(8,128)(2,1)} %param.9) | copy-start | bytes 82948
  1.4 6.7 %collective-permute-start = (bf16[4,1,8,256]{3,2,1,0:T(8,128)(2,1)S(1)}, bf16[4,1,8,256]{3,2,1,0:T(8,128)(2,1)S(1)}, u32[]{:S(2)}, u32[]{:S(2)}) collective-permute-start(bf16[4,1,8,256]{3,2,1,0:T(8,128)(2,1)S(1)} %get-tuple-element.60), channel_id=1, source_target_pairs={{0,1},{1,2},{2,3},{3,4},{4,5},{5,6},{6,7},{7,8},{8,9},{9,10},{10,1... | collective-permute-start | bytes 49160 | tf_op jit(solution)/shard_map/ppermute | solution.py:13
  5.4 4.5 collective-permute-start.1
  11.3 6.3 %copy-start.12 = (f32[16]{0:T(128)S(1)}, f32[16]{0:T(128)}, u32[]{:S(2)}) copy-start(f32[16]{0:T(128)} %param.8) | copy-start | bytes 196
  11.3 6.3 %copy-start.16 = (bf16[16,4,3,3,3]{0,1,4,3,2:T(4,128)(2,1)S(1)}, bf16[16,4,3,3,3]{0,1,4,3,2:T(4,128)(2,1)}, u32[]{:S(2)}) copy-start(bf16[16,4,3,3,3]{0,1,4,3,2:T(4,128)(2,1)} %param.7) | copy-start | bytes 10372
  11.3 6.3 %copy-start.17 = (pred[8,33]{0,1:T(8,128)(4,1)S(1)}, pred[8,33]{0,1:T(8,128)(4,1)}, u32[]{:S(2)}) copy-start(pred[8,33]{0,1:T(8,128)(4,1)} %constant.43) | copy-start | bytes 796
  55.0 4.9 %copy-start.2 = (f32[8,8,1,264,16]{3,4,1,0,2:T(8,128)}, f32[8,8,1,264,16]{3,4,1,0,2:T(8,128)S(1)}, u32[]{:S(2)}) copy-start(f32[8,8,1,264,16]{3,4,1,0,2:T(8,128)S(1)} %reshape.99) | copy-start | bytes 3244036
  59.9 18.8 %copy-start.8 = (bf16[1,4,8,8,256]{4,3,2,1,0:T(8,128)(2,1)S(1)}, bf16[1,4,8,8,256]{4,3,2,1,0:T(8,128)(2,1)}, u32[]{:S(2)}) copy-start(bf16[1,4,8,8,256]{4,3,2,1,0:T(8,128)(2,1)} %param.6) | copy-start | bytes 393220
  73.6 53.4 %collective-permute-start.2 = (bf16[16,1,4,128]{0,3,2,1:T(8,128)(2,1)}, bf16[16,1,4,128]{0,3,2,1:T(8,128)(2,1)}, u32[]{:S(2)}, u32[]{:S(2)}) collective-permute-start(bf16[16,1,4,128]{0,3,2,1:T(8,128)(2,1)} %get-tuple-element.58), channel_id=1, source_target_pairs={{0,1},{1,2},{2,3},{3,4},{4,5},{5,6},{6,7},{7,8},{8,9},{9,10},{10,1... | collective-permute-start | bytes 49160 | tf_op jit(solution)/shard_map/ppermute | solution.py:13
  77.5 50.5 %collective-permute-start.3 = (bf16[16,1,4,128]{0,3,2,1:T(8,128)(2,1)}, bf16[16,1,4,128]{0,3,2,1:T(8,128)(2,1)S(1)}, u32[]{:S(2)}, u32[]{:S(2)}) collective-permute-start(bf16[16,1,4,128]{0,3,2,1:T(8,128)(2,1)} %get-tuple-element.59), channel_id=1, source_target_pairs={{1,0},{2,1},{3,2},{4,3},{5,4},{6,5},{7,6},{8,7},{9,8},{10,9},{11,1... | collective-permute-start | bytes 49160 | tf_op jit(solution)/shard_map/ppermute | solution.py:16
  92.7 4.6 copy-start.6
  128.0 4.0 copy-start.11
  128.0 4.0 copy-start.18
  134.9 2.7 copy-start.7
  140.2 24.7 %collective-permute-start.4 = (bf16[32,1,4,128]{0,2,3,1:T(4,128)(2,1)S(1)}, bf16[32,1,4,128]{0,2,3,1:T(4,128)(2,1)S(1)}, u32[]{:S(2)}, u32[]{:S(2)}) collective-permute-start(bf16[32,1,4,128]{0,2,3,1:T(4,128)(2,1)S(1)} %get-tuple-element.56), channel_id=1, source_target_pairs={{0,1},{1,2},{2,3},{3,4},{4,5},{5,6},{6,7},{7,8},{8,9},{9,10},{10,1... | collective-permute-start | bytes 98312 | tf_op jit(solution)/shard_map/ppermute | solution.py:13
  144.2 20.8 %collective-permute-start.5 = (bf16[32,1,4,128]{0,2,3,1:T(4,128)(2,1)S(1)}, bf16[32,1,4,128]{0,2,3,1:T(4,128)(2,1)S(1)}, u32[]{:S(2)}, u32[]{:S(2)}) collective-permute-start(bf16[32,1,4,128]{0,2,3,1:T(4,128)(2,1)S(1)} %get-tuple-element.57), channel_id=1, source_target_pairs={{1,0},{2,1},{3,2},{4,3},{5,4},{6,5},{7,6},{8,7},{9,8},{10,9},{11,1... | collective-permute-start | bytes 98312 | tf_op jit(solution)/shard_map/ppermute | solution.py:16
  171.1 4.1 copy-start.15
  185.1 5.2 %copy-start.3 = (f32[8,8,1,264,16]{3,4,1,0,2:T(8,128)S(1)}, f32[8,8,1,264,16]{3,4,1,0,2:T(8,128)}, u32[]{:S(2)}) copy-start(f32[8,8,1,264,16]{3,4,1,0,2:T(8,128)} %copy-done.2) | copy-start | bytes 3244036
  185.1 5.2 %copy-start.13 = (f32[16]{0:T(128)S(1)}, f32[16]{0:T(128)}, u32[]{:S(2)}) copy-start(f32[16]{0:T(128)} %param.8) | copy-start | bytes 196
  204.9 8.7 %copy-start.4 = (bf16[16,1,8,8,256]{0,1,4,3,2:T(2,128)(2,1)S(1)}, bf16[16,1,8,8,256]{0,1,4,3,2:T(2,128)(2,1)}, u32[]{:S(2)}) copy-start(bf16[16,1,8,8,256]{0,1,4,3,2:T(2,128)(2,1)} %copy.177) | copy-start | bytes 1572868
  213.5 183.4 %copy-start.9 = (f32[32,16,3,3,3]{0,1,4,3,2:T(8,128)S(1)}, f32[32,16,3,3,3]{0,1,4,3,2:T(8,128)}, u32[]{:S(2)}) copy-start(f32[32,16,3,3,3]{0,1,4,3,2:T(8,128)} %fusion.44) | copy-start | bytes 165892
  213.5 183.4 %copy-start.10 = (f32[16]{0:T(128)S(1)}, f32[16]{0:T(128)}, u32[]{:S(2)}) copy-start(f32[16]{0:T(128)} %convert_reduce_fusion) | copy-start | bytes 196
  213.5 183.4 %copy-start.14 = (f32[32]{0:T(128)S(1)}, f32[32]{0:T(128)}, u32[]{:S(2)}) copy-start(f32[32]{0:T(128)} %get-tuple-element.52) | copy-start | bytes 388
  213.5 274.0 %copy-start.5 = (bf16[1,16,4,4,128]{1,4,3,2,0:T(8,128)(2,1)S(1)}, bf16[1,16,4,4,128]{1,4,3,2,0:T(8,128)(2,1)}, u32[]{:S(2)}) copy-start(bf16[1,16,4,4,128]{1,4,3,2,0:T(8,128)(2,1)} %get-tuple-element.55) | copy-start | bytes 196612
  213.5 274.9 %copy-start.1 = (bf16[32,16,3,3,3]{0,1,4,3,2:T(8,128)(2,1)S(1)}, bf16[32,16,3,3,3]{0,1,4,3,2:T(8,128)(2,1)}, u32[]{:S(2)}) copy-start(bf16[32,16,3,3,3]{0,1,4,3,2:T(8,128)(2,1)} %param.9) | copy-start | bytes 82948
where the time goes:
time: 497 us; the launch traced here: 489 us
  matrix products  231 us (46%)
  local copies, waits for them, and re-layouts  120 us (24%)
  blocking collectives  88.3 us (18%)
  other arithmetic  30.4 us (6%)
  starting transfers between devices  15.9 us (3%)
    transpose x2, matrix products, kernel_grad(): return result.transpose(1, 0, 2, 3, 4)  200 us
    psum x1, blocking collectives, shards(): first_terms = lax.psum((first_terms[0], first_terms[1]), ('dp', 'space'))  88.3 us
    conv_general_dilated x15, local copies, waits for them, and re-layouts, convolve(): lax.conv_general_dilated(padded[None], kernel, (1, 1, 1), 'VALID', dimens...  32.9 us
    broadcast_in_dim x2, local copies, waits for them, and re-layouts, kernel_grad(): padded[:, None]  32.2 us
    conv_general_dilated x3, matrix products, convolve(): lax.conv_general_dilated(padded[None], kernel, (1, 1, 1), 'VALID', dimens...  31.4 us
    convert_element_type x1, local copies, waits for them, and re-layouts, shards(): delta_one = (spread_up(stored_grad.astype(jnp.float32)) * 0.125 * rectify...  14.3 us
    reduce_sum x1, other arithmetic, mean_pool(): return jnp.sum(blocks, axis=(2, 4, 6)) * 0.125  12.8 us
    select_n x3, local copies, waits for them, and re-layouts, rectify_slope(): return jnp.where(values > 0, 1.0, 0.3)  12.6 us
  transfers between devices with their start and end apart: 6, of which 1 were waited for; matrix products, arithmetic and copies ran while one was open for 14% of the time, Pallas kernels for 0%

commit v1 on v0

--- a/solution.py
+++ b/solution.py
@@ -97,7 +97,7 @@
         kernel_grad(first_in, delta_one),
         jnp.sum(delta_one.astype(jnp.float32), axis=(1, 2, 3)),
     )
-    first_terms = lax.psum((first_terms[0], first_terms[1]), ("dp", "space"))
+    first_terms = lax.psum(lax.psum((first_terms[0], first_terms[1]), "dp"), "space")
     totals = (first_terms[0], first_terms[1], second_terms[0], second_terms[1])
     count_one = (
         lax.axis_size("dp") * lax.axis_size("space") * planes * sample.shape[2] * sample.shape[3]

time: 497 us -> 653 us (1.31)
  the two profiles are of different devices: /device:TPU:1 before, /device:TPU:0 now
where the time goes in v1:
time: 653 us; the launch traced here: 644 us
  blocking collectives  246 us (38%)
  matrix products  230 us (35%)
  local copies, waits for them, and re-layouts  120 us (18%)
  other arithmetic  29.9 us (5%)
  starting transfers between devices  11.4 us (2%)
    transpose x2, matrix products, kernel_grad(): return result.transpose(1, 0, 2, 3, 4)  198 us
    psum x1, blocking collectives, shards(): lax.psum((first_terms[0], first_terms[1]), 'dp')  86.2 us
    psum x1, blocking collectives, shards(): second_terms = lax.psum((second_terms[0], second_terms[1]), ('dp', 'space'))  83.1 us
    psum x1, blocking collectives, shards(): lax.psum(lax.psum((first_terms[0], first_terms[1]), 'dp'), 'space')  76.8 us
    conv_general_dilated x15, local copies, waits for them, and re-layouts, convolve(): lax.conv_general_dilated(padded[None], kernel, (1, 1, 1), 'VALID', dimens...  33.2 us
    broadcast_in_dim x2, local copies, waits for them, and re-layouts, kernel_grad(): padded[:, None]  32.5 us
    conv_general_dilated x3, matrix products, convolve(): lax.conv_general_dilated(padded[None], kernel, (1, 1, 1), 'VALID', dimens...  31.4 us
    convert_element_type x1, local copies, waits for them, and re-layouts, shards(): delta_one = (spread_up(stored_grad.astype(jnp.float32)) * 0.125 * rectify...  14.2 us
  transfers between devices with their start and end apart: 6, of which 2 were waited for; matrix products, arithmetic and copies ran while one was open for 8% of the time, Pallas kernels for 0%

profile of v1, /device:TPU:0, one launch (start us, length us, event | category | flops | bytes accessed | tf_op | source)
XLA Modules:
  0.0 644.2 jit_solution(17288703745636573418)
XLA Ops:
  1.4 1.7 collective-permute-start
  4.5 1.3 copy.164
  5.8 3.0 collective-permute-done.1
  11.0 4.3 copy.155
  16.4 25.4 %fusion = (f32[8,8,8,33,16]{4,2,3,1,0:T(8,128)}, f32[8,8,8,33,16]{4,2,3,1,0:T(8,128)}) fusion(f32[16]{0:T(128)S(1)} %copy-done.11, bf16[16,4,3,3,3]{0,1,4,3,2:T(4,128)(2,1)S(1)} %copy-done.13, bf16[4,10,10,1,7,2]{4,0,5,2,1,3:T(4,128)(2,1)S(1)} %slice.34, bf16[4,10,10,1,8,33]{4,0,5,2,1,3:T(4,128)(2,1)} %copy.155, pred[8,33]{0,1:T(8,128)(4,1)S(1)} %copy-done.14), kind=kOutput, calls=%fused_computation.2 | convolution fusion | flops 60145920 | bytes 2388872 | tf_op jit(solution)/shard_map/conv_general_dilated | solution.py:22
  41.9 8.6 %copy.156 = f32[8,8,8,33,16]{3,2,4,1,0:T(8,128)} copy(f32[8,8,8,33,16]{4,2,3,1,0:T(8,128)} %get-tuple-element.67) | data formatting | bytes 2162688 | tf_op jit(solution)/shard_map/conv_general_dilated | solution.py:22
  50.4 3.5 reshape.99
  54.0 4.8 copy.157
  58.9 12.8 %fusion.2 = f32[16,4,4,128]{0,3,2,1:T(8,128)S(1)} fusion(f32[16,4,2,4,2,128,2]{0,6,5,4,3,2,1:T(2,128)} %bitcast.110, f32[16]{0:T(128)S(1)} %copy-done.11), kind=kLoop, calls=%fused_computation.6 | loop fusion | flops 1277952 | bytes 1179712 | tf_op jit(solution)/shard_map/reduce_sum | solution.py:59
  72.5 4.1 collective-permute-start.2
  79.3 9.0 %copy.178 = f32[8,8,8,33,16]{3,2,4,1,0:T(8,128)} copy(f32[8,8,8,33,16]{4,2,3,1,0:T(8,128)} %get-tuple-element.66) | data formatting | bytes 2162688 | tf_op jit(solution)/shard_map/jit(_where)/select_n | solution.py:53
  88.3 3.5 reshape.117
  91.9 4.6 copy.190
  96.5 29.8 %copy.176 = bf16[4,1,10,10,258]{0,1,4,3,2:T(2,128)(2,1)} copy(bf16[4,1,10,10,258]{4,3,2,0,1:T(8,128)(2,1)S(1)} %copy-done.6) | data formatting | bytes 412800 | tf_op jit(solution)/shard_map/broadcast_in_dim | solution.py:34
  129.2 2.0 copy.162
  131.3 2.8 fusion.36
  136.3 2.8 copy.180
  139.0 15.5 %fusion.44 = f32[32,16,3,3,3]{0,1,4,3,2:T(8,128)S(1)} fusion(bf16[16,1,6,6,130]{0,1,4,3,2:T(2,128)(2,1)S(1)} %copy.180, bf16[32,1,4,4,128]{0,3,4,2,1:T(4,128)(2,1)} %fusion.40), kind=kOutput, calls=%fused_computation.64 | convolution fusion | flops 56623104 | bytes 336128 | tf_op jit(solution)/shard_map/transpose | solution.py:41
  154.6 83.1 %all-reduce.3 = (f32[32,16,3,3,3]{0,1,4,3,2:T(8,128)S(1)}, f32[32]{0:T(128)S(1)}) all-reduce(f32[32,16,3,3,3]{0,1,4,3,2:T(8,128)S(1)} %fusion.44, f32[32]{0:T(128)S(1)} %get-tuple-element.54), channel_id=1, replica_groups=mesh['dp'=16,'space'=16] {'dp','space'}, use_global_device_ids=true, to_apply=%region_6.7 | all-reduce | flops 13856 | bytes 110848 | tf_op jit(solution)/shard_map/psum | solution.py:89
  238.5 1.7 collective-permute-start.4
  240.2 1.3 collective-permute-start.5
  244.7 2.3 collective-permute-done.5
  247.5 2.1 reshape.111
  249.5 3.0 copy.170
  253.5 3.2 fusion.18
  260.1 7.4 %broadcast_in_dim.50 = f32[16,4,2,4,2,128,2]{0,6,5,4,3,2,1:T(2,128)} broadcast(f32[16,4,4,128]{0,3,2,1:T(8,128)S(1)} %convert_multiply_fusion), dimensions={0,1,3,5} | broadcast | bytes 1179648 | tf_op jit(solution)/shard_map/broadcast_in_dim | solution.py:64
  267.5 5.2 copy.175
  273.0 14.2 %copy.177 = bf16[16,1,8,8,256]{0,1,4,3,2:T(2,128)(2,1)} copy(bf16[16,1,8,8,256]{4,0,3,2,1:T(8,128)(2,1)S(1)} %multiply_convert_fusion) | data formatting | bytes 1048576 | tf_op jit(solution)/shard_map/convert_element_type | solution.py:95
  287.2 8.6 %convert_reduce_fusion = f32[16]{0:T(128)} fusion(f32[1,16,8,8,256]{1,4,3,2,0:T(8,128)} %bitcast.109, f32[8,8,1,256,16]{4,3,1,0,2:T(8,128)} %copy.190), kind=kLoop, calls=%fused_computation.5 | loop fusion | flops 1048560 | bytes 2097216 | tf_op jit(solution)/shard_map/reduce_sum | solution.py:98
  295.8 182.9 %fusion.81 = f32[16,4,3,3,3]{0,1,4,3,2:T(4,128)S(1)} fusion(bf16[4,1,10,10,258]{0,1,4,3,2:T(2,128)(2,1)} %copy.176, bf16[16,1,8,8,256]{0,1,4,3,2:T(2,128)(2,1)S(1)} %copy-done.4), kind=kOutput, calls=%fused_computation.118 | convolution fusion | flops 56623104 | bytes 737600 | tf_op jit(solution)/shard_map/transpose | solution.py:41
  478.8 86.2 %all-reduce.5 = (f32[16,4,3,3,3]{0,1,4,3,2:T(4,128)S(1)}, f32[16]{0:T(128)S(1)}) all-reduce(f32[16,4,3,3,3]{0,1,4,3,2:T(4,128)S(1)} %fusion.81, f32[16]{0:T(128)S(1)} %copy-done.9), channel_id=1, replica_groups=mesh['dp'=16,'space'=16] {'dp'}, use_global_device_ids=true, to_apply=%region_1.2 | all-reduce | flops 1744 | bytes 13952 | tf_op jit(solution)/shard_map/psum | solution.py:100
  565.0 76.8 %all-reduce.4 = (f32[16,4,3,3,3]{0,1,4,3,2:T(4,128)S(1)}, f32[16]{0:T(128)S(1)}) all-reduce(f32[16,4,3,3,3]{0,1,4,3,2:T(4,128)S(1)} %get-tuple-element.52, f32[16]{0:T(128)S(1)} %get-tuple-element.53), channel_id=1, replica_groups=mesh['dp'=16,'space'=16] {'space'}, use_global_device_ids=true, to_apply=%region_2.3 | all-reduce | flops 1744 | bytes 13952 | tf_op jit(solution)/shard_map/psum | solution.py:100
  (81 shorter events, 25.2 us)
Async XLA Ops:
  0.6 130.7 %copy-start = (bf16[32,16,3,3,3]{0,1,4,3,2:T(8,128)(2,1)S(1)}, bf16[32,16,3,3,3]{0,1,4,3,2:T(8,128)(2,1)}, u32[]{:S(2)}) copy-start(bf16[32,16,3,3,3]{0,1,4,3,2:T(8,128)(2,1)} %param.9) | copy-start | bytes 82948
  1.4 4.4 collective-permute-start
  3.2 5.6 collective-permute-start.1
  10.2 6.2 copy-start.11
  10.2 6.2 copy-start.13
  10.2 6.2 copy-start.14
  53.9 5.0 copy-start.2
  58.9 19.1 %copy-start.8 = (bf16[1,4,8,8,256]{4,3,2,1,0:T(8,128)(2,1)S(1)}, bf16[1,4,8,8,256]{4,3,2,1,0:T(8,128)(2,1)}, u32[]{:S(2)}) copy-start(bf16[1,4,8,8,256]{4,3,2,1,0:T(8,128)(2,1)} %param.6) | copy-start | bytes 393220
  72.5 53.8 %collective-permute-start.2 = (bf16[16,1,4,128]{0,3,2,1:T(8,128)(2,1)}, bf16[16,1,4,128]{0,3,2,1:T(8,128)(2,1)}, u32[]{:S(2)}, u32[]{:S(2)}) collective-permute-start(bf16[16,1,4,128]{0,3,2,1:T(8,128)(2,1)} %get-tuple-element.60), channel_id=1, source_target_pairs={{0,1},{1,2},{2,3},{3,4},{4,5},{5,6},{6,7},{7,8},{8,9},{9,10},{10,1... | collective-permute-start | bytes 49160 | tf_op jit(solution)/shard_map/ppermute | solution.py:13
  76.6 50.6 %collective-permute-start.3 = (bf16[16,1,4,128]{0,3,2,1:T(8,128)(2,1)}, bf16[16,1,4,128]{0,3,2,1:T(8,128)(2,1)S(1)}, u32[]{:S(2)}, u32[]{:S(2)}) collective-permute-start(bf16[16,1,4,128]{0,3,2,1:T(8,128)(2,1)} %get-tuple-element.61), channel_id=1, source_target_pairs={{1,0},{2,1},{3,2},{4,3},{5,4},{6,5},{7,6},{8,7},{9,8},{10,9},{11,1... | collective-permute-start | bytes 49160 | tf_op jit(solution)/shard_map/ppermute | solution.py:16
  91.9 4.6 copy-start.6
  127.3 4.0 copy-start.10
  127.3 4.0 copy-start.15
  134.1 2.2 copy-start.7
  238.5 6.1 collective-permute-start.4
  240.2 6.9 %collective-permute-start.5 = (bf16[32,1,4,128]{0,2,3,1:T(4,128)(2,1)S(1)}, bf16[32,1,4,128]{0,2,3,1:T(4,128)(2,1)S(1)}, u32[]{:S(2)}, u32[]{:S(2)}) collective-permute-start(bf16[32,1,4,128]{0,2,3,1:T(4,128)(2,1)S(1)} %get-tuple-element.59), channel_id=1, source_target_pairs={{1,0},{2,1},{3,2},{4,3},{5,4},{6,5},{7,6},{8,7},{9,8},{10,9},{11,1... | collective-permute-start | bytes 98312 | tf_op jit(solution)/shard_map/ppermute | solution.py:16
  253.5 4.1 copy-start.12
  267.5 5.2 copy-start.3
  287.2 8.7 %copy-start.4 = (bf16[16,1,8,8,256]{0,1,4,3,2:T(2,128)(2,1)S(1)}, bf16[16,1,8,8,256]{0,1,4,3,2:T(2,128)(2,1)}, u32[]{:S(2)}) copy-start(bf16[16,1,8,8,256]{0,1,4,3,2:T(2,128)(2,1)} %copy.177) | copy-start | bytes 1572868
  295.8 183.0 %copy-start.9 = (f32[16]{0:T(128)S(1)}, f32[16]{0:T(128)}, u32[]{:S(2)}) copy-start(f32[16]{0:T(128)} %convert_reduce_fusion) | copy-start | bytes 196
  295.8 347.1 %copy-start.5 = (bf16[1,16,4,4,128]{1,4,3,2,0:T(8,128)(2,1)S(1)}, bf16[1,16,4,4,128]{1,4,3,2,0:T(8,128)(2,1)}, u32[]{:S(2)}) copy-start(bf16[1,16,4,4,128]{1,4,3,2,0:T(8,128)(2,1)} %get-tuple-element.57) | copy-start | bytes 196612
  295.8 348.0 %copy-start.1 = (bf16[32,16,3,3,3]{0,1,4,3,2:T(8,128)(2,1)S(1)}, bf16[32,16,3,3,3]{0,1,4,3,2:T(8,128)(2,1)}, u32[]{:S(2)}) copy-start(bf16[32,16,3,3,3]{0,1,4,3,2:T(8,128)(2,1)} %param.9) | copy-start | bytes 82948
